TPU v7x, 256 devices: a whole 4x4x8 slice. The times are simulated.
256 devices in a mesh: span: 8 (over z_lo, y), ulysses: 32 (over x, z_hi, core).
Axes of the slice: x: 4, y: 4, z: 8 (z_hi: 4, z_lo: 2; z = z_hi * 2 + z_lo), core: 2. Of those that a mesh axis runs over, the one named last changes fastest.
Arguments:
- query: bfloat16 [32768, 4096], P(('span', 'ulysses')), may hold values from -32 to 32
- key: bfloat16 [32768, 1024], P(('span', 'ulysses')), may hold values from -6 to 6
- value: bfloat16 [32768, 1024], P(('span', 'ulysses')), may hold values from -6 to 6
- d_out: bfloat16 [32768, 4096], P(('span', 'ulysses')), may hold values from -6 to 6
Outputs:
- attended: bfloat16 [32768, 4096], P(('span', 'ulysses'))
- grad_query: float32 [1024, 4096], P(('span', 'ulysses'))
- grad_key: float32 [1024, 1024], P(('span', 'ulysses'))
- grad_value: float32 [1024, 1024], P(('span', 'ulysses'))
All inputs are finite; a program needn't handle non-finite values.
Results may differ from a plain program's by a relative error of at most 0.0048.
Values may be sent and summed in bfloat16 or wider, within the bound.
A program may use at most 256 MiB of HBM per device.

v0:
```python
import math
import jax
import jax.numpy as jnp
from jax import lax
from jax.sharding import PartitionSpec as P

H = 32
HD = 128
KVH = 8
INTERVAL = 32


def widen(field):
    count = field.shape[0]
    repeat = H // KVH
    spread = jnp.broadcast_to(field.reshape(count, KVH, 1, HD), (count, KVH, repeat, HD))
    return spread.reshape(count, H * HD)


def on_device(query, key, value, d_out):
    tok_rows = query.shape[0]
    n_heads_axis = lax.axis_size("ulysses")
    span_len = tok_rows * n_heads_axis
    per_dev = H // n_heads_axis
    beacons = span_len // INTERVAL
    beacon_dev = tok_rows // INTERVAL
    scale = 1.0 / math.sqrt(HD)
    q_h, k_h, v_h, g_h = (
        lax.all_to_all(query, "ulysses", split_axis=1, concat_axis=0, tiled=True),
        lax.all_to_all(widen(key), "ulysses", split_axis=1, concat_axis=0, tiled=True),
        lax.all_to_all(widen(value), "ulysses", split_axis=1, concat_axis=0, tiled=True),
        lax.all_to_all(d_out, "ulysses", split_axis=1, concat_axis=0, tiled=True),
    )
    own_k = k_h.reshape(beacons, INTERVAL, per_dev * HD)[:, -1]
    own_v = v_h.reshape(beacons, INTERVAL, per_dev * HD)[:, -1]
    prior_k, prior_v = (
        lax.all_gather(own_k, "span", axis=0, tiled=True),
        lax.all_gather(own_v, "span", axis=0, tiled=True),
    )
    all_beacons = prior_k.shape[0]
    mine = lax.axis_index("span")
    visible = jnp.arange(all_beacons) // beacons < mine
    q3 = q_h.reshape(span_len, per_dev, HD)
    k3 = k_h.reshape(span_len, per_dev, HD)
    v3 = v_h.reshape(span_len, per_dev, HD)
    g3 = g_h.reshape(span_len, per_dev, HD)
    pk3 = prior_k.reshape(all_beacons, per_dev, HD)
    pv3 = prior_v.reshape(all_beacons, per_dev, HD)
    own_v3 = v3.reshape(beacons, INTERVAL, per_dev, HD)[:, -1]
    dk_prior = jnp.zeros((all_beacons, per_dev, HD), jnp.float32)
    dv_prior = jnp.zeros((all_beacons, per_dev, HD), jnp.float32)
    dk_own = jnp.zeros((beacons, per_dev, HD), jnp.float32)
    dv_own = jnp.zeros((beacons, per_dev, HD), jnp.float32)
    out_blocks = []
    dq_blocks = []
    block = min(512, span_len)
    n_rows = block // INTERVAL
    for index in range(span_len // block):
        first = index * block
        upper = first + block
        q_blk = q3[first:upper]
        g_blk = g3[first:upper]
        k_loc = k3[:upper]
        v_loc = v3[:upper]
        s_prior = jnp.einsum("qhd,khd->hqk", q_blk, pk3, preferred_element_type=jnp.float32) * scale
        s_prior = jnp.where(visible[None, None, :], s_prior, -jnp.inf)
        s_local = (
            jnp.einsum("qhd,khd->hqk", q_blk, k_loc, preferred_element_type=jnp.float32) * scale
        )
        causal = jnp.arange(upper)[None, :] <= (first + jnp.arange(block))[:, None]
        s_local = jnp.where(causal[None], s_local, -jnp.inf)
        peak = jnp.maximum(jnp.max(s_prior, axis=2), jnp.max(s_local, axis=2))
        e_prior = jnp.exp(s_prior - peak[:, :, None])
        e_local = jnp.exp(s_local - peak[:, :, None])
        denom = jnp.sum(e_prior, axis=2) + jnp.sum(e_local, axis=2)
        p_prior = e_prior / denom[:, :, None]
        p_local = e_local / denom[:, :, None]
        b_prior = p_prior.astype(jnp.bfloat16)
        b_local = p_local.astype(jnp.bfloat16)
        attended = jnp.einsum("hqk,khd->qhd", b_prior, pv3, preferred_element_type=jnp.float32)
        attended = attended + jnp.einsum(
            "hqk,khd->qhd", b_local, v_loc, preferred_element_type=jnp.float32
        )
        out_b = attended.astype(jnp.bfloat16)
        out_blocks.append(out_b)
        delta = jnp.sum(g_blk.astype(jnp.float32) * out_b.astype(jnp.float32), axis=2).T
        dp_prior = jnp.einsum("qhd,khd->hqk", g_blk, pv3, preferred_element_type=jnp.float32)
        ds_prior = (p_prior * (dp_prior - delta[:, :, None])).astype(jnp.bfloat16)
        dk_prior = (
            dk_prior
            + jnp.einsum("hqk,qhd->khd", ds_prior, q_blk, preferred_element_type=jnp.float32)
            * scale
        )
        dv_prior = dv_prior + jnp.einsum(
            "hqk,qhd->khd", b_prior, g_blk, preferred_element_type=jnp.float32
        )
        n_own = upper // INTERVAL
        p_own = p_local.reshape(per_dev, block, n_own, INTERVAL)[..., -1]
        b_own = b_local.reshape(per_dev, block, n_own, INTERVAL)[..., -1]
        dp_own = jnp.einsum(
            "qhd,khd->hqk", g_blk, own_v3[:n_own], preferred_element_type=jnp.float32
        )
        ds_own = (p_own * (dp_own - delta[:, :, None])).astype(jnp.bfloat16)
        dk_own = dk_own.at[:n_own].add(
            jnp.einsum("hqk,qhd->khd", ds_own, q_blk, preferred_element_type=jnp.float32) * scale
        )
        dv_own = dv_own.at[:n_own].add(
            jnp.einsum("hqk,qhd->khd", b_own, g_blk, preferred_element_type=jnp.float32)
        )
        ds_rows_prior = ds_prior.reshape(per_dev, n_rows, INTERVAL, all_beacons)[:, :, -1]
        p_rows_local = p_local.reshape(per_dev, n_rows, INTERVAL, upper)[:, :, -1]
        g_rows = g_blk.reshape(n_rows, INTERVAL, per_dev, HD)[:, -1]
        delta_rows = delta.reshape(per_dev, n_rows, INTERVAL)[:, :, -1]
        dp_rows = jnp.einsum("qhd,khd->hqk", g_rows, v_loc, preferred_element_type=jnp.float32)
        ds_rows_local = (p_rows_local * (dp_rows - delta_rows[:, :, None])).astype(jnp.bfloat16)
        dq_rows = jnp.einsum("hqk,khd->qhd", ds_rows_prior, pk3, preferred_element_type=jnp.float32)
        dq_rows = dq_rows + jnp.einsum(
            "hqk,khd->qhd", ds_rows_local, k_loc, preferred_element_type=jnp.float32
        )
        dq_blocks.append(dq_rows * scale)
    out_heads = jnp.concatenate(out_blocks, 0).reshape(span_len, per_dev * HD)
    attended_tokens = lax.all_to_all(out_heads, "ulysses", split_axis=0, concat_axis=1, tiled=True)
    stacked = jnp.stack(
        [dk_prior.reshape(all_beacons, per_dev * HD), dv_prior.reshape(all_beacons, per_dev * HD)],
        1,
    )
    from_later = lax.psum_scatter(stacked, "span", scatter_dimension=0, tiled=True)
    grad_k_heads = dk_own.reshape(beacons, per_dev * HD) + from_later[:, 0]
    grad_v_heads = dv_own.reshape(beacons, per_dev * HD) + from_later[:, 1]
    grad_q_heads = jnp.concatenate(dq_blocks, 0).reshape(beacons, per_dev * HD)
    grad_q_tok, grad_k_tok, grad_v_tok = (
        lax.all_to_all(grad_q_heads, "ulysses", split_axis=0, concat_axis=1, tiled=True),
        lax.all_to_all(grad_k_heads, "ulysses", split_axis=0, concat_axis=1, tiled=True),
        lax.all_to_all(grad_v_heads, "ulysses", split_axis=0, concat_axis=1, tiled=True),
    )
    repeat = H // KVH
    grad_k_tok = (
        grad_k_tok.reshape(beacon_dev, KVH, repeat, HD).sum(axis=2).reshape(beacon_dev, KVH * HD)
    )
    grad_v_tok = (
        grad_v_tok.reshape(beacon_dev, KVH, repeat, HD).sum(axis=2).reshape(beacon_dev, KVH * HD)
    )
    return (attended_tokens, grad_q_tok, grad_k_tok, grad_v_tok)


def solution(mesh):
    return jax.shard_map(
        on_device,
        mesh=mesh,
        in_specs=(
            P(("span", "ulysses"), None),
            P(("span", "ulysses"), None),
            P(("span", "ulysses"), None),
            P(("span", "ulysses"), None),
        ),
        out_specs=(
            P(("span", "ulysses"), None),
            P(("span", "ulysses"), None),
            P(("span", "ulysses"), None),
            P(("span", "ulysses"), None),
        ),
        check_vma=False,
    )
```

profile of v0, /device:TPU:9, one launch (start us, length us, event | category | flops | bytes accessed | tf_op | source)
XLA Modules:
  0.0 729.1 jit_solution(17974472516163867103)
XLA Ops:
  9.4 11.8 %all-to-all-start.2 = ((bf16[128,32,128]{2,0,1:T(8,128)(2,1)}), bf16[128,32,128]{2,0,1:T(8,128)(2,1)S(1)}, u32[]{:S(2)}, u32[]{:S(2)}) async-start(bf16[128,32,128]{2,0,1:T(8,128)(2,1)} %bitcast.8), calls=%async_computation.2 | async-start | bytes 2097152 | tf_op jit(solution)/shard_map/all_to_all | solution.py:31
  21.2 28.5 %all-to-all-done.2 = bf16[128,32,128]{2,0,1:T(8,128)(2,1)S(1)} async-done(((bf16[128,32,128]{2,0,1:T(8,128)(2,1)}), bf16[128,32,128]{2,0,1:T(8,128)(2,1)S(1)}, u32[]{:S(2)}, u32[]{:S(2)}) %all-to-all-start.2) | async-done | bytes 1048608 | tf_op jit(solution)/shard_map/all_to_all | solution.py:31
  58.2 26.2 %all-to-all-done.1 = bf16[128,32,128]{2,0,1:T(8,128)(2,1)S(1)} async-done(((bf16[128,32,128]{2,0,1:T(8,128)(2,1)}), bf16[128,32,128]{2,0,1:T(8,128)(2,1)S(1)}, u32[]{:S(2)}, u32[]{:S(2)}) %all-to-all-start.1) | async-done | bytes 1048608 | tf_op jit(solution)/shard_map/all_to_all | solution.py:30
  95.7 35.9 %all-gather.1 = bf16[1024,1,128]{2,0,1:T(8,128)(2,1)S(1)} all-gather(bf16[128,1,128]{2,0,1:T(8,128)(2,1)S(1)} %copy.230), channel_id=3, replica_groups=mesh['span'=8,'ulysses'=32] {'span'}, dimensions={0}, use_global_device_ids=true | all-gather | bytes 294912 | tf_op jit(solution)/shard_map/all_gather | solution.py:38
  131.6 14.3 %all-to-all-start.4 = ((bf16[128,32,128]{0,2,1:T(8,128)(2,1)}), bf16[128,32,128]{0,2,1:T(8,128)(2,1)}, u32[]{:S(2)}, u32[]{:S(2)}) async-start(bf16[128,32,128]{0,2,1:T(8,128)(2,1)} %bitcast.868), calls=%async_computation.4 | async-start | bytes 2097152 | tf_op jit(solution)/shard_map/all_to_all | solution.py:32
  150.3 37.2 %all-gather = bf16[1024,1,128]{2,0,1:T(8,128)(2,1)S(1)} all-gather(bf16[128,1,128]{2,0,1:T(8,128)(2,1)S(1)} %copy.228), channel_id=2, replica_groups=mesh['span'=8,'ulysses'=32] {'span'}, dimensions={0}, use_global_device_ids=true | all-gather | bytes 294912 | tf_op jit(solution)/shard_map/all_gather | solution.py:37
  236.6 6.8 fusion.34
  260.8 5.8 fusion.396
  362.0 7.3 %fusion.384 = (bf16[512,2560]{1,0:T(8,128)(2,1)}, f32[512,2560]{1,0:T(8,128)}) fusion(f32[512]{0:T(512)S(1)} %add.460, f32[512,2560]{1,0:T(8,128)} %get-tuple-element.287, f32[512]{0:T(512)} %copy-done.118), kind=kLoop, calls=%fused_computation.511 | loop fusion | flops 3932160 | bytes 13111296 | tf_op jit(solution)/shard_map/convert_element_type | solution.py:79
  375.0 5.7 fusion.380
  380.9 7.2 fusion.378
  389.8 5.6 fusion.390
  464.4 6.0 copy.296
  481.3 6.5 copy.297
  542.8 5.9 copy.285
  558.0 6.7 copy.286
  576.0 8.5 %copy.287 = f32[512,3584]{0,1:T(8,128)} copy(f32[512,3584]{1,0:T(8,128)} %get-tuple-element.232) | data formatting | bytes 14680064 | tf_op jit(solution)/shard_map/div | solution.py:77
  596.4 9.0 %copy.288 = f32[512,4096]{0,1:T(8,128)} copy(f32[512,4096]{1,0:T(8,128)} %get-tuple-element.230) | data formatting | bytes 16777216 | tf_op jit(solution)/shard_map/div | solution.py:77
  624.6 17.0 %all-to-all-start.5 = ((f32[32,4,128]{2,1,0:T(4,128)}), f32[32,4,128]{2,1,0:T(4,128)S(1)}, u32[]{:S(2)}, u32[]{:S(2)}) async-start(f32[32,4,128]{2,1,0:T(4,128)} %bitcast.974), calls=%async_computation.5 | async-start | bytes 131072 | tf_op jit(solution)/shard_map/all_to_all | solution.py:132
  653.2 9.8 %all-to-all-start.3 = ((bf16[32,128,128]{2,1,0:T(8,128)(2,1)}), bf16[32,128,128]{2,1,0:T(8,128)(2,1)S(1)}, u32[]{:S(2)}, u32[]{:S(2)}) async-start(bf16[32,128,128]{2,1,0:T(8,128)(2,1)} %bitcast.964), calls=%async_computation.3 | async-start | bytes 2097152 | tf_op jit(solution)/shard_map/all_to_all | solution.py:122
  673.6 18.0 %all-to-all-done.3 = bf16[32,128,128]{2,1,0:T(8,128)(2,1)S(1)} async-done(((bf16[32,128,128]{2,1,0:T(8,128)(2,1)}), bf16[32,128,128]{2,1,0:T(8,128)(2,1)S(1)}, u32[]{:S(2)}, u32[]{:S(2)}) %all-to-all-start.3) | async-done | bytes 1048608 | tf_op jit(solution)/shard_map/all_to_all | solution.py:122
  691.6 5.7 all-to-all-start.7
  699.2 7.8 %all-to-all-done.7 = f32[32,4,128]{2,1,0:T(4,128)S(1)} async-done(((f32[32,4,128]{2,1,0:T(4,128)}), f32[32,4,128]{2,1,0:T(4,128)S(1)}, u32[]{:S(2)}, u32[]{:S(2)}) %all-to-all-start.7) | async-done | bytes 65568 | tf_op jit(solution)/shard_map/all_to_all | solution.py:134
  712.7 8.1 %all-to-all-done.6 = f32[32,4,128]{2,1,0:T(4,128)S(1)} async-done(((f32[32,4,128]{2,1,0:T(4,128)}), f32[32,4,128]{2,1,0:T(4,128)S(1)}, u32[]{:S(2)}, u32[]{:S(2)}) %all-to-all-start.6) | async-done | bytes 65568 | tf_op jit(solution)/shard_map/all_to_all | solution.py:133
  (642 shorter events, 411.7 us)
Async XLA Ops:
  9.4 40.4 %all-to-all-start.2 = ((bf16[128,32,128]{2,0,1:T(8,128)(2,1)}), bf16[128,32,128]{2,0,1:T(8,128)(2,1)S(1)}, u32[]{:S(2)}, u32[]{:S(2)}) async-start(bf16[128,32,128]{2,0,1:T(8,128)(2,1)} %bitcast.8), calls=%async_computation.2 | async-start | bytes 2097152 | tf_op jit(solution)/shard_map/all_to_all | solution.py:31
  51.0 33.4 %all-to-all-start.1 = ((bf16[128,32,128]{2,0,1:T(8,128)(2,1)}), bf16[128,32,128]{2,0,1:T(8,128)(2,1)S(1)}, u32[]{:S(2)}, u32[]{:S(2)}) async-start(bf16[128,32,128]{2,0,1:T(8,128)(2,1)} %bitcast.867), calls=%async_computation.1 | async-start | bytes 2097152 | tf_op jit(solution)/shard_map/all_to_all | solution.py:30
  84.3 47.3 %all-to-all-start = ((bf16[128,32,128]{0,2,1:T(8,128)(2,1)}), bf16[128,32,128]{0,2,1:T(8,128)(2,1)}, u32[]{:S(2)}, u32[]{:S(2)}) async-start(bf16[128,32,128]{0,2,1:T(8,128)(2,1)} %bitcast.869), calls=%async_computation | async-start | bytes 2097152 | tf_op jit(solution)/shard_map/all_to_all | solution.py:29
  91.9 144.6 %copy-start.156 = (pred[1024]{0:T(1024)(128)(4,1)}, pred[1024]{0:T(1024)(128)(4,1)S(1)}, u32[]{:S(2)}) copy-start(pred[1024]{0:T(1024)(128)(4,1)S(1)} %fusion.338) | copy-start | bytes 3076
  95.7 52.7 %copy-start.106 = (bf16[4,128,128]{2,1,0:T(8,128)(2,1)}, bf16[4,128,128]{2,1,0:T(8,128)(2,1)S(1)}, u32[]{:S(2)}) copy-start(bf16[4,128,128]{2,1,0:T(8,128)(2,1)S(1)} %slice.786) | copy-start | bytes 393220
  131.6 96.7 %all-to-all-start.4 = ((bf16[128,32,128]{0,2,1:T(8,128)(2,1)}), bf16[128,32,128]{0,2,1:T(8,128)(2,1)}, u32[]{:S(2)}, u32[]{:S(2)}) async-start(bf16[128,32,128]{0,2,1:T(8,128)(2,1)} %bitcast.868), calls=%async_computation.4 | async-start | bytes 2097152 | tf_op jit(solution)/shard_map/all_to_all | solution.py:32
  145.9 526.0 %reduce-scatter.2.cloned.1.call-start = ((), (), s32[]{:S(2)}) async-start(), calls=%async_computation.9 | async-start | bytes 1179648 | tf_op jit(solution)/shard_map/reduce_scatter | solution.py:127
  236.5 30.1 %copy-start.32 = (f32[512,1024]{1,0:T(8,128)}, f32[512,1024]{1,0:T(8,128)S(1)}, u32[]{:S(2)}) copy-start(f32[512,1024]{1,0:T(8,128)S(1)} %get-tuple-element.279) | copy-start | bytes 6291460
  244.4 30.2 %copy-start.127 = (f32[512]{0:T(512)}, f32[512]{0:T(512)S(1)}, u32[]{:S(2)}) copy-start(f32[512]{0:T(512)S(1)} %max.74) | copy-start | bytes 6148
  252.4 76.9 %copy-start.118 = (f32[512]{0:T(512)}, f32[512]{0:T(512)S(1)}, u32[]{:S(2)}) copy-start(f32[512]{0:T(512)S(1)} %max.76) | copy-start | bytes 6148
  256.4 77.0 %copy-start.120 = (f32[512]{0:T(512)}, f32[512]{0:T(512)S(1)}, u32[]{:S(2)}) copy-start(f32[512]{0:T(512)S(1)} %max.77) | copy-start | bytes 6148
  260.7 77.1 %copy-start.122 = (f32[512]{0:T(512)}, f32[512]{0:T(512)S(1)}, u32[]{:S(2)}) copy-start(f32[512]{0:T(512)S(1)} %max.78) | copy-start | bytes 6148
  623.4 28.4 %copy-start.51 = (bf16[4,128,128]{2,1,0:T(8,128)(2,1)S(1)}, bf16[4,128,128]{2,1,0:T(8,128)(2,1)}, u32[]{:S(2)}) copy-start(bf16[4,128,128]{2,1,0:T(8,128)(2,1)} %copy.245) | copy-start | bytes 393220
  623.5 28.6 %copy-start.39 = (bf16[4,128,128]{2,1,0:T(8,128)(2,1)S(1)}, bf16[4,128,128]{2,1,0:T(8,128)(2,1)}, u32[]{:S(2)}) copy-start(bf16[4,128,128]{2,1,0:T(8,128)(2,1)} %copy.250) | copy-start | bytes 393220
  623.5 28.6 %copy-start.112 = (bf16[1,512,48,1]{1,3,2,0:T(2,128)(2,1)S(1)}, bf16[1,512,48,1]{1,3,2,0:T(2,128)(2,1)}, u32[]{:S(2)}) copy-start(bf16[1,512,48,1]{1,3,2,0:T(2,128)(2,1)} %slice.873) | copy-start | bytes 147460
  624.6 28.0 %all-to-all-start.5 = ((f32[32,4,128]{2,1,0:T(4,128)}), f32[32,4,128]{2,1,0:T(4,128)S(1)}, u32[]{:S(2)}, u32[]{:S(2)}) async-start(f32[32,4,128]{2,1,0:T(4,128)} %bitcast.974), calls=%async_computation.5 | async-start | bytes 131072 | tf_op jit(solution)/shard_map/all_to_all | solution.py:132
  653.2 38.4 %all-to-all-start.3 = ((bf16[32,128,128]{2,1,0:T(8,128)(2,1)}), bf16[32,128,128]{2,1,0:T(8,128)(2,1)S(1)}, u32[]{:S(2)}, u32[]{:S(2)}) async-start(bf16[32,128,128]{2,1,0:T(8,128)(2,1)} %bitcast.964), calls=%async_computation.3 | async-start | bytes 2097152 | tf_op jit(solution)/shard_map/all_to_all | solution.py:122
  663.1 34.3 %copy-start.58 = (bf16[4,128,128]{2,1,0:T(8,128)(2,1)S(1)}, bf16[4,128,128]{2,1,0:T(8,128)(2,1)}, u32[]{:S(2)}) copy-start(bf16[4,128,128]{2,1,0:T(8,128)(2,1)} %copy.237) | copy-start | bytes 393220
  665.4 31.9 %copy-start.113 = (bf16[128,1,1,128]{3,1,0,2:T(2,128)(2,1)S(1)}, bf16[128,1,1,128]{3,1,0,2:T(2,128)(2,1)}, u32[]{:S(2)}) copy-start(bf16[128,1,1,128]{3,1,0,2:T(2,128)(2,1)} %slice.868) | copy-start | bytes 98308
  665.4 31.9 %copy-start.134 = (f32[512]{0:T(512)S(1)}, f32[512]{0:T(512)}, u32[]{:S(2)}) copy-start(f32[512]{0:T(512)} %copy-done.133) | copy-start | bytes 6148
  671.5 49.9 %copy-start.111 = (f32[32,4,128]{2,1,0:T(4,128)S(1)}, f32[32,4,128]{2,1,0:T(4,128)}, u32[]{:S(2)}) copy-start(f32[32,4,128]{2,1,0:T(4,128)} %copy-done.110) | copy-start | bytes 196612
  671.5 50.5 %copy-start.1 = (bf16[128,1024]{1,0:T(8,128)(2,1)S(1)}, bf16[128,1024]{1,0:T(8,128)(2,1)}, u32[]{:S(2)}) copy-start(bf16[128,1024]{1,0:T(8,128)(2,1)} %param.42) | copy-start | bytes 786436
  691.6 15.5 %all-to-all-start.7 = ((f32[32,4,128]{2,1,0:T(4,128)}), f32[32,4,128]{2,1,0:T(4,128)S(1)}, u32[]{:S(2)}, u32[]{:S(2)}) async-start(f32[32,4,128]{2,1,0:T(4,128)} %bitcast.242), calls=%async_computation.8 | async-start | bytes 131072 | tf_op jit(solution)/shard_map/all_to_all | solution.py:134
  707.1 13.8 %all-to-all-start.6 = ((f32[32,4,128]{2,1,0:T(4,128)}), f32[32,4,128]{2,1,0:T(4,128)S(1)}, u32[]{:S(2)}, u32[]{:S(2)}) async-start(f32[32,4,128]{2,1,0:T(4,128)} %bitcast.204), calls=%async_computation.7 | async-start | bytes 131072 | tf_op jit(solution)/shard_map/all_to_all | solution.py:133
  (168 other events, 1143.7 us)
Sparse Core Ops, SparseCore 0:
  595.7 43.3 reduce-scatter.1
where the time goes:
time: 741 us; the launch traced here: 729 us
  local copies, waits for them, and re-layouts  236 us (32%)
  matrix products  165 us (22%)
  waiting for transfers between devices  88.7 us (12%)
  other arithmetic  77.3 us (10%)
  blocking collectives  73.2 us (10%)
  starting transfers between devices  72.7 us (10%)
  between operations  16.1 us (2%)
    div x8, local copies, waits for them, and re-layouts, on_device(): p_local = e_local / denom[:, :, None]  45.1 us
    convert_element_type x8, other arithmetic, on_device(): b_local = p_local.astype(jnp.bfloat16)  40.5 us
    all_gather x1, blocking collectives, on_device(): lax.all_gather(own_k, 'span', axis=0, tiled=True)  37.2 us
    all_gather x1, blocking collectives, on_device(): lax.all_gather(own_v, 'span', axis=0, tiled=True)  35.9 us
    convert_element_type x7, local copies, waits for them, and re-layouts, on_device(): b_local = p_local.astype(jnp.bfloat16)  30.5 us
    all_to_all x1, waiting for transfers between devices, on_device(): lax.all_to_all(widen(value), 'ulysses', split_axis=1, concat_axis=0, tile...  28.5 us
    all_to_all x1, waiting for transfers between devices, on_device(): lax.all_to_all(widen(key), 'ulysses', split_axis=1, concat_axis=0, tiled=...  26.2 us
    dot_general x8, matrix products, on_device(): jnp.einsum('hqk,khd->qhd', b_local, v_loc, preferred_element_type=jnp.flo...  24.8 us
  transfers between devices with their start and end apart: 9, of which 5 were waited for; matrix products, arithmetic and copies ran while one was open for 15% of the time, Pallas kernels for 0%

commit v1 on v0

--- a/solution.py
+++ b/solution.py
@@ -8,6 +8,13 @@
 HD = 128
 KVH = 8
 INTERVAL = 32
+
+
+def all_by_exchange(x, axis, d):
+    size = lax.axis_size(axis)
+    tiles = jnp.stack([x for _ in range(size)])
+    tiles = lax.all_to_all(tiles, axis, split_axis=0, concat_axis=0)
+    return jnp.concatenate(tiles, axis=d)
 
 
 def widen(field):
@@ -34,7 +41,7 @@
     own_k = k_h.reshape(beacons, INTERVAL, per_dev * HD)[:, -1]
     own_v = v_h.reshape(beacons, INTERVAL, per_dev * HD)[:, -1]
     prior_k, prior_v = (
-        lax.all_gather(own_k, "span", axis=0, tiled=True),
+        all_by_exchange(own_k, "span", 0),
         lax.all_gather(own_v, "span", axis=0, tiled=True),
     )
     all_beacons = prior_k.shape[0]

time: 741 us -> 699 us (0.943)
  blocking collectives: 73.2 us -> 24 us
  waiting for transfers between devices: 88.7 us -> 108 us
    all_gather x1 -> x0, blocking collectives: 37.2 us -> none  [on_device(): lax.all_gather(own_k, 'span', axis=0, tiled=True)]
    all_to_all x1, waiting for transfers between devices: 0.01 us -> 23.2 us  [on_device(): lax.all_to_all(query, 'ulysses', split_axis=1, concat_axis=0, tiled=True)]
    dot_general x8, matrix products: 20.3 us -> 7.03 us  [on_device(): jnp.einsum('qhd,khd->hqk', q_blk, pk3, preferred_element_type=jnp.float32)]
    all_gather x1, blocking collectives: 35.9 us -> 24 us  [on_device(): lax.all_gather(own_v, 'span', axis=0, tiled=True)]
    dot_general x8, matrix products: 22.1 us -> 30.8 us  [on_device(): jnp.einsum('qhd,khd->hqk', q_blk, k_loc, preferred_element_type=jnp.float32)]
    unnamed x369 -> x376, local copies, waits for them, and re-layouts: 20 us -> 18.2 us
  transfers between devices with their start and end apart: 9 -> 10, of which waited for: 5 -> 6; matrix products, arithmetic and copies ran while one was open for 15% -> 23% of each run, Pallas kernels for 0% -> 0%
where the time goes in v1:
time: 699 us; the launch traced here: 689 us
  local copies, waits for them, and re-layouts  234 us (33%)
  matrix products  160 us (23%)
  waiting for transfers between devices  108 us (15%)
  starting transfers between devices  74 us (11%)
  other arithmetic  71.9 us (10%)
  blocking collectives  24 us (3%)
  between operations  16.2 us (2%)
    div x8, local copies, waits for them, and re-layouts, on_device(): p_local = e_local / denom[:, :, None]  44.8 us
    convert_element_type x8, other arithmetic, on_device(): b_local = p_local.astype(jnp.bfloat16)  42.7 us
    dot_general x8, matrix products, on_device(): jnp.einsum('qhd,khd->hqk', q_blk, k_loc, preferred_element_type=jnp.float32)  30.8 us
    convert_element_type x7, local copies, waits for them, and re-layouts, on_device(): b_local = p_local.astype(jnp.bfloat16)  30.4 us
    all_to_all x1, waiting for transfers between devices, on_device(): lax.all_to_all(widen(value), 'ulysses', split_axis=1, concat_axis=0, tile...  28.5 us
    all_to_all x1, waiting for transfers between devices, on_device(): lax.all_to_all(widen(key), 'ulysses', split_axis=1, concat_axis=0, tiled=...  26.2 us
    dot_general x8, matrix products, on_device(): jnp.einsum('hqk,khd->qhd', b_local, v_loc, preferred_element_type=jnp.flo...  24.7 us
    dot_general x8, matrix products, on_device(): jnp.einsum('qhd,khd->hqk', g_blk, pv3, preferred_element_type=jnp.float32)  24.1 us
  transfers between devices with their start and end apart: 10, of which 6 were waited for; matrix products, arithmetic and copies ran while one was open for 23% of the time, Pallas kernels for 0%

profile of v1, /device:TPU:9, one launch (start us, length us, event | category | flops | bytes accessed | tf_op | source)
XLA Modules:
  0.0 688.8 jit_solution(9515768144443243157)
XLA Ops:
  9.4 11.8 %all-to-all-start.3 = ((bf16[128,32,128]{2,0,1:T(8,128)(2,1)}), bf16[128,32,128]{2,0,1:T(8,128)(2,1)S(1)}, u32[]{:S(2)}, u32[]{:S(2)}) async-start(bf16[128,32,128]{2,0,1:T(8,128)(2,1)} %bitcast.8), calls=%async_computation.3 | async-start | bytes 2097152 | tf_op jit(solution)/shard_map/all_to_all | solution.py:38
  21.2 28.5 %all-to-all-done.3 = bf16[128,32,128]{2,0,1:T(8,128)(2,1)S(1)} async-done(((bf16[128,32,128]{2,0,1:T(8,128)(2,1)}), bf16[128,32,128]{2,0,1:T(8,128)(2,1)S(1)}, u32[]{:S(2)}, u32[]{:S(2)}) %all-to-all-start.3) | async-done | bytes 1048608 | tf_op jit(solution)/shard_map/all_to_all | solution.py:38
  58.2 26.2 %all-to-all-done.1 = bf16[128,32,128]{2,0,1:T(8,128)(2,1)S(1)} async-done(((bf16[128,32,128]{2,0,1:T(8,128)(2,1)}), bf16[128,32,128]{2,0,1:T(8,128)(2,1)S(1)}, u32[]{:S(2)}, u32[]{:S(2)}) %all-to-all-start.1) | async-done | bytes 1048608 | tf_op jit(solution)/shard_map/all_to_all | solution.py:37
  91.9 23.2 %all-to-all-done = bf16[128,32,128]{0,2,1:T(8,128)(2,1)} async-done(((bf16[128,32,128]{0,2,1:T(8,128)(2,1)}), bf16[128,32,128]{0,2,1:T(8,128)(2,1)}, u32[]{:S(2)}, u32[]{:S(2)}) %all-to-all-start) | async-done | bytes 1048608 | tf_op jit(solution)/shard_map/all_to_all | solution.py:36
  115.1 8.1 %all-to-all-start.5 = ((bf16[128,32,128]{0,2,1:T(8,128)(2,1)}), bf16[128,32,128]{0,2,1:T(8,128)(2,1)}, u32[]{:S(2)}, u32[]{:S(2)}) async-start(bf16[128,32,128]{0,2,1:T(8,128)(2,1)} %bitcast.873), calls=%async_computation.5 | async-start | bytes 2097152 | tf_op jit(solution)/shard_map/all_to_all | solution.py:39
  154.8 24.0 %all-gather = bf16[1024,1,128]{2,0,1:T(8,128)(2,1)S(1)} all-gather(bf16[128,1,128]{2,0,1:T(8,128)(2,1)} %copy.229), channel_id=2, replica_groups=mesh['span'=8,'ulysses'=32] {'span'}, dimensions={0}, use_global_device_ids=true | all-gather | bytes 294912 | tf_op jit(solution)/shard_map/all_gather | solution.py:45
  252.1 5.5 fusion.372
  290.5 5.8 fusion.362
  322.9 7.3 %fusion.360 = (bf16[512,2560]{1,0:T(8,128)(2,1)}, f32[512,2560]{1,0:T(8,128)}) fusion(f32[512]{0:T(512)S(1)} %add.460, f32[512,2560]{1,0:T(8,128)} %get-tuple-element.287, f32[512]{0:T(512)} %copy-done.113), kind=kLoop, calls=%fused_computation.488 | loop fusion | flops 3932160 | bytes 13111296 | tf_op jit(solution)/shard_map/convert_element_type | solution.py:86
  341.9 7.2 %fusion.354 = (bf16[512,4096]{1,0:T(8,128)(2,1)}, f32[512,4096]{1,0:T(8,128)}) fusion(f32[512]{0:T(512)S(1)} %add.472, f32[512,4096]{1,0:T(8,128)S(1)} %bitcast.824, f32[512]{0:T(512)S(1)} %copy-done.121), kind=kLoop, calls=%fused_computation.485 | loop fusion | flops 6291456 | bytes 20975616 | tf_op jit(solution)/shard_map/convert_element_type | solution.py:86
  350.8 5.6 fusion.366
  425.4 5.9 copy.295
  442.2 6.5 copy.296
  487.0 5.7 copy.283
  503.4 5.9 copy.284
  518.6 6.6 copy.285
  536.6 8.5 %copy.286 = f32[512,3584]{0,1:T(8,128)} copy(f32[512,3584]{1,0:T(8,128)} %get-tuple-element.232) | data formatting | bytes 14680064 | tf_op jit(solution)/shard_map/div | solution.py:84
  556.9 9.0 %copy.287 = f32[512,4096]{0,1:T(8,128)} copy(f32[512,4096]{1,0:T(8,128)} %get-tuple-element.230) | data formatting | bytes 16777216 | tf_op jit(solution)/shard_map/div | solution.py:84
  585.2 17.0 %all-to-all-start.6 = ((f32[32,4,128]{2,1,0:T(4,128)}), f32[32,4,128]{2,1,0:T(4,128)S(1)}, u32[]{:S(2)}, u32[]{:S(2)}) async-start(f32[32,4,128]{2,1,0:T(4,128)} %bitcast.980), calls=%async_computation.6 | async-start | bytes 131072 | tf_op jit(solution)/shard_map/all_to_all | solution.py:139
  613.8 9.8 %all-to-all-start.4 = ((bf16[32,128,128]{2,1,0:T(8,128)(2,1)}), bf16[32,128,128]{2,1,0:T(8,128)(2,1)S(1)}, u32[]{:S(2)}, u32[]{:S(2)}) async-start(bf16[32,128,128]{2,1,0:T(8,128)(2,1)} %bitcast.969), calls=%async_computation.4 | async-start | bytes 2097152 | tf_op jit(solution)/shard_map/all_to_all | solution.py:129
  634.2 14.4 %all-to-all-done.4 = bf16[32,128,128]{2,1,0:T(8,128)(2,1)S(1)} async-done(((bf16[32,128,128]{2,1,0:T(8,128)(2,1)}), bf16[32,128,128]{2,1,0:T(8,128)(2,1)S(1)}, u32[]{:S(2)}, u32[]{:S(2)}) %all-to-all-start.4) | async-done | bytes 1048608 | tf_op jit(solution)/shard_map/all_to_all | solution.py:129
  648.6 8.3 %all-to-all-start.8 = ((f32[32,4,128]{2,1,0:T(4,128)}), f32[32,4,128]{2,1,0:T(4,128)S(1)}, u32[]{:S(2)}, u32[]{:S(2)}) async-start(f32[32,4,128]{2,1,0:T(4,128)} %bitcast.242), calls=%async_computation.9 | async-start | bytes 131072 | tf_op jit(solution)/shard_map/all_to_all | solution.py:141
  658.8 7.8 %all-to-all-done.8 = f32[32,4,128]{2,1,0:T(4,128)S(1)} async-done(((f32[32,4,128]{2,1,0:T(4,128)}), f32[32,4,128]{2,1,0:T(4,128)S(1)}, u32[]{:S(2)}, u32[]{:S(2)}) %all-to-all-start.8) | async-done | bytes 65568 | tf_op jit(solution)/shard_map/all_to_all | solution.py:141
  672.3 8.1 %all-to-all-done.7 = f32[32,4,128]{2,1,0:T(4,128)S(1)} async-done(((f32[32,4,128]{2,1,0:T(4,128)}), f32[32,4,128]{2,1,0:T(4,128)S(1)}, u32[]{:S(2)}, u32[]{:S(2)}) %all-to-all-start.7) | async-done | bytes 65568 | tf_op jit(solution)/shard_map/all_to_all | solution.py:140
  (652 shorter events, 405.9 us)
Async XLA Ops:
  9.4 40.4 %all-to-all-start.3 = ((bf16[128,32,128]{2,0,1:T(8,128)(2,1)}), bf16[128,32,128]{2,0,1:T(8,128)(2,1)S(1)}, u32[]{:S(2)}, u32[]{:S(2)}) async-start(bf16[128,32,128]{2,0,1:T(8,128)(2,1)} %bitcast.8), calls=%async_computation.3 | async-start | bytes 2097152 | tf_op jit(solution)/shard_map/all_to_all | solution.py:38
  51.0 33.4 %all-to-all-start.1 = ((bf16[128,32,128]{2,0,1:T(8,128)(2,1)}), bf16[128,32,128]{2,0,1:T(8,128)(2,1)S(1)}, u32[]{:S(2)}, u32[]{:S(2)}) async-start(bf16[128,32,128]{2,0,1:T(8,128)(2,1)} %bitcast.872), calls=%async_computation.1 | async-start | bytes 2097152 | tf_op jit(solution)/shard_map/all_to_all | solution.py:37
  84.3 30.7 %all-to-all-start = ((bf16[128,32,128]{0,2,1:T(8,128)(2,1)}), bf16[128,32,128]{0,2,1:T(8,128)(2,1)}, u32[]{:S(2)}, u32[]{:S(2)}) async-start(bf16[128,32,128]{0,2,1:T(8,128)(2,1)} %bitcast.874), calls=%async_computation | async-start | bytes 2097152 | tf_op jit(solution)/shard_map/all_to_all | solution.py:36
  115.1 63.7 %all-to-all-start.5 = ((bf16[128,32,128]{0,2,1:T(8,128)(2,1)}), bf16[128,32,128]{0,2,1:T(8,128)(2,1)}, u32[]{:S(2)}, u32[]{:S(2)}) async-start(bf16[128,32,128]{0,2,1:T(8,128)(2,1)} %bitcast.873), calls=%async_computation.5 | async-start | bytes 2097152 | tf_op jit(solution)/shard_map/all_to_all | solution.py:39
  123.2 138.9 %copy-start.150 = (pred[1024]{0:T(1024)(128)(4,1)}, pred[1024]{0:T(1024)(128)(4,1)S(1)}, u32[]{:S(2)}) copy-start(pred[1024]{0:T(1024)(128)(4,1)S(1)} %fusion.314) | copy-start | bytes 3076
  180.3 77.3 %all-to-all-start.2 = ((bf16[8,128,128]{2,1,0:T(8,128)(2,1)}), bf16[8,128,128]{2,1,0:T(8,128)(2,1)S(1)}, u32[]{:S(2)}, u32[]{:S(2)}) async-start(bf16[8,128,128]{2,1,0:T(8,128)(2,1)} %stack.6), calls=%async_computation.2 | async-start | bytes 524288 | tf_op jit(solution)/shard_map/all_to_all | solution.py:16
  184.9 447.6 %reduce-scatter.2.cloned.1.call-start = ((), (), s32[]{:S(2)}) async-start(), calls=%async_computation.10 | async-start | bytes 1179648 | tf_op jit(solution)/shard_map/reduce_scatter | solution.py:134
  268.8 31.5 %copy-start.115 = (f32[512]{0:T(512)}, f32[512]{0:T(512)S(1)}, u32[]{:S(2)}) copy-start(f32[512]{0:T(512)S(1)} %max.77) | copy-start | bytes 6148
  268.9 33.1 %copy-start.117 = (f32[512]{0:T(512)}, f32[512]{0:T(512)S(1)}, u32[]{:S(2)}) copy-start(f32[512]{0:T(512)S(1)} %max.78) | copy-start | bytes 6148
  584.0 28.5 %copy-start.47 = (bf16[4,128,128]{2,1,0:T(8,128)(2,1)S(1)}, bf16[4,128,128]{2,1,0:T(8,128)(2,1)}, u32[]{:S(2)}) copy-start(bf16[4,128,128]{2,1,0:T(8,128)(2,1)} %copy.244) | copy-start | bytes 393220
  584.0 28.5 %copy-start.89 = (f32[128,1,128]{2,0,1:T(8,128)S(1)}, f32[128,1,128]{2,0,1:T(8,128)}, u32[]{:S(2)}) copy-start(f32[128,1,128]{2,0,1:T(8,128)} %scatter-add.59) | copy-start | bytes 196612
  584.0 28.6 %copy-start.35 = (bf16[4,128,128]{2,1,0:T(8,128)(2,1)S(1)}, bf16[4,128,128]{2,1,0:T(8,128)(2,1)}, u32[]{:S(2)}) copy-start(bf16[4,128,128]{2,1,0:T(8,128)(2,1)} %copy.249) | copy-start | bytes 393220
  585.2 27.6 %copy-start.103 = (bf16[1,512,64,1]{1,3,2,0:T(2,128)(2,1)S(1)}, bf16[1,512,64,1]{1,3,2,0:T(2,128)(2,1)}, u32[]{:S(2)}) copy-start(bf16[1,512,64,1]{1,3,2,0:T(2,128)(2,1)} %slice.875) | copy-start | bytes 196612
  585.2 27.8 %copy-start.43 = (bf16[4,128,128]{2,1,0:T(8,128)(2,1)S(1)}, bf16[4,128,128]{2,1,0:T(8,128)(2,1)}, u32[]{:S(2)}) copy-start(bf16[4,128,128]{2,1,0:T(8,128)(2,1)} %copy.259) | copy-start | bytes 393220
  585.2 27.8 %copy-start.102 = (bf16[1,512,80,1]{1,3,2,0:T(2,128)(2,1)S(1)}, bf16[1,512,80,1]{1,3,2,0:T(2,128)(2,1)}, u32[]{:S(2)}) copy-start(bf16[1,512,80,1]{1,3,2,0:T(2,128)(2,1)} %slice.877) | copy-start | bytes 245764
  585.2 28.0 %all-to-all-start.6 = ((f32[32,4,128]{2,1,0:T(4,128)}), f32[32,4,128]{2,1,0:T(4,128)S(1)}, u32[]{:S(2)}, u32[]{:S(2)}) async-start(f32[32,4,128]{2,1,0:T(4,128)} %bitcast.980), calls=%async_computation.6 | async-start | bytes 131072 | tf_op jit(solution)/shard_map/all_to_all | solution.py:139
  613.8 34.8 %all-to-all-start.4 = ((bf16[32,128,128]{2,1,0:T(8,128)(2,1)}), bf16[32,128,128]{2,1,0:T(8,128)(2,1)S(1)}, u32[]{:S(2)}, u32[]{:S(2)}) async-start(bf16[32,128,128]{2,1,0:T(8,128)(2,1)} %bitcast.969), calls=%async_computation.4 | async-start | bytes 2097152 | tf_op jit(solution)/shard_map/all_to_all | solution.py:129
  623.6 33.3 %copy-start.55 = (bf16[4,128,128]{2,1,0:T(8,128)(2,1)S(1)}, bf16[4,128,128]{2,1,0:T(8,128)(2,1)}, u32[]{:S(2)}) copy-start(bf16[4,128,128]{2,1,0:T(8,128)(2,1)} %copy.236) | copy-start | bytes 393220
  626.0 31.0 %copy-start.108 = (bf16[128,1,1,128]{3,1,0,2:T(2,128)(2,1)S(1)}, bf16[128,1,1,128]{3,1,0,2:T(2,128)(2,1)}, u32[]{:S(2)}) copy-start(bf16[128,1,1,128]{3,1,0,2:T(2,128)(2,1)} %slice.868) | copy-start | bytes 98308
  626.0 31.0 %copy-start.129 = (f32[512]{0:T(512)S(1)}, f32[512]{0:T(512)}, u32[]{:S(2)}) copy-start(f32[512]{0:T(512)} %copy-done.128) | copy-start | bytes 6148
  632.1 48.9 %copy-start.106 = (f32[32,4,128]{2,1,0:T(4,128)S(1)}, f32[32,4,128]{2,1,0:T(4,128)}, u32[]{:S(2)}) copy-start(f32[32,4,128]{2,1,0:T(4,128)} %copy-done.105) | copy-start | bytes 196612
  632.1 49.6 %copy-start.1 = (bf16[128,1024]{1,0:T(8,128)(2,1)S(1)}, bf16[128,1024]{1,0:T(8,128)(2,1)}, u32[]{:S(2)}) copy-start(bf16[128,1024]{1,0:T(8,128)(2,1)} %param.42) | copy-start | bytes 786436
  648.6 18.0 %all-to-all-start.8 = ((f32[32,4,128]{2,1,0:T(4,128)}), f32[32,4,128]{2,1,0:T(4,128)S(1)}, u32[]{:S(2)}, u32[]{:S(2)}) async-start(f32[32,4,128]{2,1,0:T(4,128)} %bitcast.242), calls=%async_computation.9 | async-start | bytes 131072 | tf_op jit(solution)/shard_map/all_to_all | solution.py:141
  666.7 13.7 %all-to-all-start.7 = ((f32[32,4,128]{2,1,0:T(4,128)}), f32[32,4,128]{2,1,0:T(4,128)S(1)}, u32[]{:S(2)}, u32[]{:S(2)}) async-start(f32[32,4,128]{2,1,0:T(4,128)} %bitcast.204), calls=%async_computation.8 | async-start | bytes 131072 | tf_op jit(solution)/shard_map/all_to_all | solution.py:140
  (172 other events, 1069.6 us)
Sparse Core Ops, SparseCore 0:
  556.3 43.1 reduce-scatter.1
